TPU v7x, 32 devices: a whole 2x2x4 slice. The times are simulated.
32 devices in a mesh: space: 4 (over y, core), vel: 8 (over z, x).
Axes of the slice: x: 2, y: 2, z: 4, core: 2. Of those that a mesh axis runs over, the one named last changes fastest.
Arguments:
- distribution: float32 [64, 48, 2304], P('space', 'vel'), may hold values from 0 to 2
- collision_rate: float32 [64], P('space'), may hold values from 0.1 to 1
- face_flags: int32 [64], replicated, may hold values 0 or 1
Outputs:
- updated: float32 [64, 48, 2304], P('space', 'vel')
All inputs are finite; a program needn't handle non-finite values.
Results may differ from a plain program's by a relative error of at most 0.0001.
Values sent between devices are 32-bit elements; how exact they have to be, the bound alone decides.
A program may use at most 64 MiB of HBM per device.

v0:
```python
import math
import jax
import jax.numpy as jnp
from jax import lax
from jax.sharding import PartitionSpec as P

NV = 48
LENGTH = 8.0
RADIUS = 6.0
COURANT = 0.9
GOLDEN = (1.0 + math.sqrt(5.0)) / 2.0
DIRECTIONS = (
    (0.0, 1.0, GOLDEN),
    (0.0, -1.0, GOLDEN),
    (1.0, GOLDEN, 0.0),
    (-1.0, GOLDEN, 0.0),
    (GOLDEN, 0.0, 1.0),
    (-GOLDEN, 0.0, 1.0),
)
HIGHEST_MODE = lax.Precision.HIGHEST


def padded_2(cells, sides, width):
    for axis, dim in sides:
        count = lax.axis_size(axis)
        ends = count - 1
        head = lax.slice_in_dim(cells, 0, width, axis=dim)
        tail = lax.slice_in_dim(cells, cells.shape[dim] - width, cells.shape[dim], axis=dim)
        cells = jnp.concatenate(
            [
                lax.ppermute(tail, axis, [(i, (i + 1) % count) for i in range(ends)]),
                cells,
                lax.ppermute(head, axis, [((i + 1) % count, i) for i in range(ends)]),
            ],
            axis=dim,
        )
    return cells


def kernel_tables(points):
    index = jnp.arange(points, dtype=jnp.int32)
    wrapped = jnp.where(
        index < points // 2, index, jnp.where(index == points // 2, 0, index - points)
    )
    signed = wrapped.astype(jnp.float32) * (math.pi / LENGTH)
    wave_x = signed[:, None, None]
    wave_y = signed[None, :, None]
    wave_z = signed[None, None, :]
    square = wave_x * wave_x + wave_y * wave_y + wave_z * wave_z
    scale = math.sqrt(1.0 + GOLDEN * GOLDEN)
    gain_tables = []
    loss_tables = []
    for direction in DIRECTIONS:
        parallel = (wave_x * direction[0] + wave_y * direction[1] + wave_z * direction[2]) / scale
        across = jnp.sqrt(jnp.maximum(square - parallel * parallel, 0.0))
        gain_tables.append(jnp.cos(0.5 * RADIUS * parallel))
        loss_tables.append(jnp.sinc(RADIUS * across / (2.0 * math.pi)))
    loss_total = sum(loss_tables) / 6.0
    return (gain_tables, loss_tables, loss_total)


def dft_tables(points):
    index = jnp.arange(points, dtype=jnp.int32)
    product = index[:, None] * index[None, :] % points
    angle = product.astype(jnp.float32) * (2.0 * math.pi / points)
    cosine = jnp.cos(angle)
    sine = jnp.sin(angle)
    first_table = jnp.stack([cosine, -sine], axis=1)
    forward_table = jnp.stack(
        [jnp.stack([cosine, -sine], axis=1), jnp.stack([sine, cosine], axis=1)], axis=1
    )
    inverse_table = jnp.stack(
        [jnp.stack([cosine, sine], axis=1), jnp.stack([-sine, cosine], axis=1)], axis=1
    )
    return (first_table, forward_table, inverse_table)


def apply_table(tensor, table, dims):
    return lax.dot_general(
        tensor,
        table,
        ((dims, tuple(range(len(dims)))), ((), ())),
        precision=HIGHEST_MODE,
        preferred_element_type=jnp.float32,
    )


def forward_cube(cube, tables):
    first_table, forward_table, inverse_table = tables
    section_one = apply_table(cube, first_table, (1,))
    section_two = apply_table(section_one, forward_table, (1, 2))
    return apply_table(section_two, forward_table, (0, 2))


def inverse_pair(spectrum, tables):
    first_table, forward_table, inverse_table = tables
    points = spectrum.shape[0]
    section_one = apply_table(spectrum, inverse_table, (3, 2))
    section_two = apply_table(section_one, inverse_table, (0, 2))
    section_three = apply_table(section_two, inverse_table, (0, 2))
    section_three = section_three * (1.0 / float(points**3))
    return (section_three[:, :, 0, :], section_three[:, :, 1, :])


def packed(spectrum, first_factor, second_factor):
    real_part = spectrum[:, :, 0, :]
    imag_part = spectrum[:, :, 1, :]
    first_factor = jnp.asarray(first_factor, jnp.float32)
    first_factor = first_factor[:, :, :] if first_factor.ndim == 3 else first_factor
    joined_real = first_factor * real_part - second_factor * imag_part
    joined_imag = first_factor * imag_part + second_factor * real_part
    return jnp.stack([joined_real, joined_imag], axis=2)


def collide(spectrum, kernels, tables):
    gain_tables, loss_tables, loss_total = kernels
    products = []
    for gain_table, loss_table in zip(gain_tables, loss_tables):
        first_part, second_part = inverse_pair(packed(spectrum, gain_table, loss_table), tables)
        products.append(first_part * second_part)
    gain_total = sum(products) / 6.0
    cube, loss_field = inverse_pair(packed(spectrum, 1.0, loss_total), tables)
    return gain_total - cube * loss_field


def body(distribution, collision_rate, face_flags):
    cell_count, planes_dev, width = distribution.shape
    points = NV
    tables = dft_tables(points)
    kernels = kernel_tables(points)

    def from_cell(one_cell):
        cube = one_cell.reshape(points, points, points)
        spectrum = forward_cube(cube, tables)
        return collide(spectrum, kernels, tables).reshape(points, width)

    regrouped = lax.all_to_all(distribution, "vel", split_axis=0, concat_axis=1, tiled=True)
    cell_terms = lax.map(from_cell, regrouped)
    collision_term = lax.all_to_all(cell_terms, "vel", split_axis=1, concat_axis=0, tiled=True)
    offset = lax.axis_index("space") * cell_count
    padded = padded_2(distribution, (("space", 0),), 1)
    mirror = distribution.reshape(cell_count, planes_dev, points, points)[:, :, ::-1, :].reshape(
        cell_count, planes_dev, width
    )
    wall_flags = jnp.concatenate([face_flags, jnp.ones((1,), jnp.int32)])
    nearby_walls = lax.dynamic_slice_in_dim(wall_flags, offset, cell_count + 1)
    lower_wall = (nearby_walls[:-1] == 1)[:, None, None]
    upper_wall = (nearby_walls[1:] == 1)[:, None, None]
    at_start = (offset + jnp.arange(cell_count, dtype=jnp.int32) == 0)[:, None, None]
    lower_side = jnp.where(lower_wall, mirror, jnp.where(at_start, distribution, padded[:-2]))
    upper_side = jnp.where(upper_wall, mirror, padded[2:])
    column = (jnp.arange(width, dtype=jnp.int32) // points).astype(jnp.float32)
    centre = (points - 1) / 2.0
    speed = COURANT * (column - centre) / centre
    upwind_flux = jnp.where(
        speed > 0, speed * (distribution - lower_side), speed * (upper_side - distribution)
    )
    return distribution - upwind_flux + collision_rate[:, None, None] * collision_term


def solution(mesh):
    return jax.shard_map(
        body,
        mesh=mesh,
        in_specs=(P("space", "vel", None), P("space"), P()),
        out_specs=P("space", "vel", None),
        check_vma=False,
    )
```

profile of v0, /device:TPU:0, one launch (start us, length us, event | category | flops | bytes accessed | tf_op | source)
XLA Modules:
  0.0 418.8 jit_solution(5220611589307567298)
XLA Ops:
  2.8 7.3 %all-to-all-start = ((f32[16,6,2304]{2,1,0:T(8,128)}), f32[16,6,2304]{2,1,0:T(8,128)S(1)}, u32[]{:S(2)}, u32[]{:S(2)}) async-start(f32[16,6,2304]{2,1,0:T(8,128)} %copy.77), calls=%async_computation | async-start | bytes 2359296 | tf_op jit(solution)/shard_map/all_to_all | solution.py:137
  10.6 13.5 %add_multiply_fusion = (f32[48,48,48]{2,1,0:T(8,128)}, f32[48,48,48]{2,1,0:T(8,128)}, f32[48,48,48]{2,1,0:T(8,128)}, f32[48,48,48]{2,1,0:T(8,128)}, f32[48,48,48...) fusion(f32[48]{0:T(128)S(1)} %get-tuple-element.737, f32[48,48]{1,0:T(8,128)S(1)} %get-tuple-element.739, ...), kind=kLoop, calls=%fused_computation.329 | loop fusion | flops 26652672 | bytes 3161856 | tf_op jit(solution)/shard_map/div | solution.py:58
  24.2 14.4 %all-to-all-done = f32[16,6,2304]{2,1,0:T(8,128)S(1)} async-done(((f32[16,6,2304]{2,1,0:T(8,128)}), f32[16,6,2304]{2,1,0:T(8,128)S(1)}, u32[]{:S(2)}, u32[]{:S(2)}) %all-to-all-start) | async-done | bytes 884768 | tf_op jit(solution)/shard_map/all_to_all | solution.py:137
  39.3 347.2 %while.13 = (s32[]{:T(128)}, f32[2,48,2304]{2,0,1:T(2,128)}, f32[2,48,2304]{2,0,1:T(2,128)S(1)}, f32[48,2,48]{2,0,1:T(8,128)S(1)}, f32[48,2,2,48]{3,0,1,2:T(8,12...) while((s32[]{:T(128)}, f32[2,48,2304]{2,0,1:T(2,128)}, ...), condition=%wide.region_1.3_spmd.clone.clone.clone, body=%wide.region_0.2_spmd.clone.clone.clone.sunk | while | flops 5998288896 | bytes 128030208 | solution.py:138
  49.0 6.0 %fusion.365 = f32[48,48,2,48,1]{0,3,4,2,1:T(8,128)S(1)} fusion(f32[48,48,2,48,1]{1,0,2,4,3:T(8,128)} %copy.170, f32[48,2,2,48]{3,0,1,2:T(8,128)S(1)} %get-tuple-element.770), kind=kOutput, calls=%fused_computation.156.clone.1 | convolution fusion | flops 254803968 | bytes 1806336 | tf_op jit(solution)/shard_map/while/body/eval_jaxpr/dot_general | solution.py:79
  57.1 10.0 %fusion.367 = (f32[48,48,1,48]{3,1,2,0:T(8,128)}, f32[48,48,1,48]{3,1,2,0:T(8,128)}, f32[48,48,1,48]{3,1,2,0:T(8,128)S(1)}, f32[48,48,1,48]{3,1,2,0:T(8,128)S(1)...) fusion(f32[48,48,48]{2,1,0:T(8,128)S(1)} %copy-done.16, f32[48]{0:T(128)S(1)} %get-tuple-element.779, ...), kind=kLoop, calls=%fused_computation.117.clone.1 | loop fusion | flops 2211840 | bytes 4884672 | tf_op jit(solution)/shard_map/while/body/eval_jaxpr/sub | solution.py:110
  74.5 6.0 %fusion.381 = f32[48,48,2,48,1]{0,3,4,2,1:T(8,128)S(1)} fusion(f32[48,48,2,48,1]{0,1,2,4,3:T(8,128)} %copy.176, f32[48,2,2,48]{3,0,1,2:T(8,128)S(1)} %get-tuple-element.772), kind=kOutput, calls=%fused_computation.148.clone.1 | convolution fusion | flops 254803968 | bytes 1806336 | tf_op jit(solution)/shard_map/while/body/eval_jaxpr/dot_general | solution.py:79
  91.4 6.0 %fusion.383 = f32[48,48,2,48,1]{0,3,4,2,1:T(8,128)S(1)} fusion(f32[48,48,2,48,1]{0,1,2,4,3:T(8,128)} %copy.177, f32[48,2,2,48]{3,0,1,2:T(8,128)S(1)} %get-tuple-element.772), kind=kOutput, calls=%fused_computation.152.clone.1 | convolution fusion | flops 254803968 | bytes 1806336 | tf_op jit(solution)/shard_map/while/body/eval_jaxpr/dot_general | solution.py:79
  101.0 9.6 %fusion.370 = (f32[48,48,1,48]{3,1,2,0:T(8,128)}, f32[48,48,1,48]{3,1,2,0:T(8,128)}, f32[48,48,1,48]{3,1,2,0:T(8,128)S(1)}, f32[48,48,1,48]{3,1,2,0:T(8,128)S(1)}) fusion(f32[48,48,48]{2,1,0:T(8,128)S(1)} %copy-done.18, f32[48]{0:T(128)S(1)} %get-tuple-element.785, f32[48,48]{1,0:T(8,128)S(1)} %copy-done.24, f32[48,48,2,48]{3,1,2,0:T(8,128)S(1)} %fusion.366, ...), kind=kLoop, calls=%fused_computation.93.clone.1 | loop fusion | flops 1769472 | bytes 3557568 | tf_op jit(solution)/shard_map/while/body/eval_jaxpr/sub | solution.py:110
  118.0 6.0 %fusion.372 = f32[48,48,2,48,1]{0,3,4,2,1:T(8,128)S(1)} fusion(f32[48,48,2,48,1]{0,1,2,4,3:T(8,128)} %copy.172, f32[48,2,2,48]{3,0,1,2:T(8,128)S(1)} %get-tuple-element.772), kind=kOutput, calls=%fused_computation.132.clone.1 | convolution fusion | flops 254803968 | bytes 1806336 | tf_op jit(solution)/shard_map/while/body/eval_jaxpr/dot_general | solution.py:79
  131.0 4.1 copy.173
  135.2 6.0 %fusion.374 = f32[48,48,2,48,1]{0,3,4,2,1:T(8,128)S(1)} fusion(f32[48,48,2,48,1]{0,1,2,4,3:T(8,128)} %copy.173, f32[48,2,2,48]{3,0,1,2:T(8,128)S(1)} %get-tuple-element.772), kind=kOutput, calls=%fused_computation.136.clone.1 | convolution fusion | flops 254803968 | bytes 1806336 | tf_op jit(solution)/shard_map/while/body/eval_jaxpr/dot_general | solution.py:79
  144.8 9.6 %fusion.375 = (f32[48,48,1,48]{3,1,2,0:T(8,128)}, f32[48,48,1,48]{3,1,2,0:T(8,128)}, f32[48,48,1,48]{3,1,2,0:T(8,128)S(1)}, f32[48,48,1,48]{3,1,2,0:T(8,128)S(1)}) fusion(f32[48,48,48]{2,1,0:T(8,128)S(1)} %copy-done.14, f32[48]{0:T(128)S(1)} %get-tuple-element.782, f32[48,48]{1,0:T(8,128)S(1)} %copy-done.26, f32[48,48,2,48]{3,1,2,0:T(8,128)S(1)} %fusion.366, ...), kind=kLoop, calls=%fused_computation.105.clone.1 | loop fusion | flops 1769472 | bytes 3557568 | tf_op jit(solution)/shard_map/while/body/eval_jaxpr/sub | solution.py:110
  159.2 6.0 %fusion.377 = f32[48,48,2,48,1]{0,3,4,2,1:T(8,128)S(1)} fusion(f32[48,48,2,48,1]{0,1,2,4,3:T(8,128)} %copy.174, f32[48,2,2,48]{3,0,1,2:T(8,128)S(1)} %get-tuple-element.772), kind=kOutput, calls=%fused_computation.140.clone.1 | convolution fusion | flops 254803968 | bytes 1806336 | tf_op jit(solution)/shard_map/while/body/eval_jaxpr/dot_general | solution.py:79
  174.7 6.0 %fusion.379 = f32[48,48,2,48,1]{0,3,4,2,1:T(8,128)S(1)} fusion(f32[48,48,2,48,1]{0,1,2,4,3:T(8,128)} %copy.175, f32[48,2,2,48]{3,0,1,2:T(8,128)S(1)} %get-tuple-element.772), kind=kOutput, calls=%fused_computation.144.clone.1 | convolution fusion | flops 254803968 | bytes 1806336 | tf_op jit(solution)/shard_map/while/body/eval_jaxpr/dot_general | solution.py:79
  191.7 6.2 %fusion.369 = f32[48,48,2,48,1]{0,3,4,2,1:T(8,128)S(1)} fusion(f32[48,48,2,48,1]{0,1,2,4,3:T(8,128)} %copy.171, f32[48,2,2,48]{3,0,1,2:T(8,128)S(1)} %get-tuple-element.772), kind=kOutput, calls=%fused_computation.128.clone.1 | convolution fusion | flops 254803968 | bytes 1806336 | tf_op jit(solution)/shard_map/while/body/eval_jaxpr/dot_general | solution.py:79
  200.2 4.2 fusion.384
  220.4 6.0 %fusion.365 = f32[48,48,2,48,1]{0,3,4,2,1:T(8,128)S(1)} fusion(f32[48,48,2,48,1]{1,0,2,4,3:T(8,128)} %copy.170, f32[48,2,2,48]{3,0,1,2:T(8,128)S(1)} %get-tuple-element.770), kind=kOutput, calls=%fused_computation.156.clone.1 | convolution fusion | flops 254803968 | bytes 1806336 | tf_op jit(solution)/shard_map/while/body/eval_jaxpr/dot_general | solution.py:79
  228.6 10.0 %fusion.367 = (f32[48,48,1,48]{3,1,2,0:T(8,128)}, f32[48,48,1,48]{3,1,2,0:T(8,128)}, f32[48,48,1,48]{3,1,2,0:T(8,128)S(1)}, f32[48,48,1,48]{3,1,2,0:T(8,128)S(1)...) fusion(f32[48,48,48]{2,1,0:T(8,128)S(1)} %copy-done.16, f32[48]{0:T(128)S(1)} %get-tuple-element.779, ...), kind=kLoop, calls=%fused_computation.117.clone.1 | loop fusion | flops 2211840 | bytes 4884672 | tf_op jit(solution)/shard_map/while/body/eval_jaxpr/sub | solution.py:110
  246.0 6.0 %fusion.381 = f32[48,48,2,48,1]{0,3,4,2,1:T(8,128)S(1)} fusion(f32[48,48,2,48,1]{0,1,2,4,3:T(8,128)} %copy.176, f32[48,2,2,48]{3,0,1,2:T(8,128)S(1)} %get-tuple-element.772), kind=kOutput, calls=%fused_computation.148.clone.1 | convolution fusion | flops 254803968 | bytes 1806336 | tf_op jit(solution)/shard_map/while/body/eval_jaxpr/dot_general | solution.py:79
  262.9 6.0 %fusion.383 = f32[48,48,2,48,1]{0,3,4,2,1:T(8,128)S(1)} fusion(f32[48,48,2,48,1]{0,1,2,4,3:T(8,128)} %copy.177, f32[48,2,2,48]{3,0,1,2:T(8,128)S(1)} %get-tuple-element.772), kind=kOutput, calls=%fused_computation.152.clone.1 | convolution fusion | flops 254803968 | bytes 1806336 | tf_op jit(solution)/shard_map/while/body/eval_jaxpr/dot_general | solution.py:79
  272.5 9.6 %fusion.370 = (f32[48,48,1,48]{3,1,2,0:T(8,128)}, f32[48,48,1,48]{3,1,2,0:T(8,128)}, f32[48,48,1,48]{3,1,2,0:T(8,128)S(1)}, f32[48,48,1,48]{3,1,2,0:T(8,128)S(1)}) fusion(f32[48,48,48]{2,1,0:T(8,128)S(1)} %copy-done.18, f32[48]{0:T(128)S(1)} %get-tuple-element.785, f32[48,48]{1,0:T(8,128)S(1)} %copy-done.24, f32[48,48,2,48]{3,1,2,0:T(8,128)S(1)} %fusion.366, ...), kind=kLoop, calls=%fused_computation.93.clone.1 | loop fusion | flops 1769472 | bytes 3557568 | tf_op jit(solution)/shard_map/while/body/eval_jaxpr/sub | solution.py:110
  285.5 4.2 %copy.172 = f32[48,48,2,48,1]{0,1,2,4,3:T(8,128)} copy(f32[48,48,2,48,1]{3,1,2,0,4:T(8,128)} %fusion.371) | data formatting | bytes 1769472 | tf_op jit(solution)/shard_map/while/body/eval_jaxpr/dot_general | solution.py:79
  289.8 6.0 %fusion.372 = f32[48,48,2,48,1]{0,3,4,2,1:T(8,128)S(1)} fusion(f32[48,48,2,48,1]{0,1,2,4,3:T(8,128)} %copy.172, f32[48,2,2,48]{3,0,1,2:T(8,128)S(1)} %get-tuple-element.772), kind=kOutput, calls=%fused_computation.132.clone.1 | convolution fusion | flops 254803968 | bytes 1806336 | tf_op jit(solution)/shard_map/while/body/eval_jaxpr/dot_general | solution.py:79
  306.6 6.0 %fusion.374 = f32[48,48,2,48,1]{0,3,4,2,1:T(8,128)S(1)} fusion(f32[48,48,2,48,1]{0,1,2,4,3:T(8,128)} %copy.173, f32[48,2,2,48]{3,0,1,2:T(8,128)S(1)} %get-tuple-element.772), kind=kOutput, calls=%fused_computation.136.clone.1 | convolution fusion | flops 254803968 | bytes 1806336 | tf_op jit(solution)/shard_map/while/body/eval_jaxpr/dot_general | solution.py:79
  316.3 9.6 %fusion.375 = (f32[48,48,1,48]{3,1,2,0:T(8,128)}, f32[48,48,1,48]{3,1,2,0:T(8,128)}, f32[48,48,1,48]{3,1,2,0:T(8,128)S(1)}, f32[48,48,1,48]{3,1,2,0:T(8,128)S(1)}) fusion(f32[48,48,48]{2,1,0:T(8,128)S(1)} %copy-done.14, f32[48]{0:T(128)S(1)} %get-tuple-element.782, f32[48,48]{1,0:T(8,128)S(1)} %copy-done.26, f32[48,48,2,48]{3,1,2,0:T(8,128)S(1)} %fusion.366, ...), kind=kLoop, calls=%fused_computation.105.clone.1 | loop fusion | flops 1769472 | bytes 3557568 | tf_op jit(solution)/shard_map/while/body/eval_jaxpr/sub | solution.py:110
  330.7 6.0 %fusion.377 = f32[48,48,2,48,1]{0,3,4,2,1:T(8,128)S(1)} fusion(f32[48,48,2,48,1]{0,1,2,4,3:T(8,128)} %copy.174, f32[48,2,2,48]{3,0,1,2:T(8,128)S(1)} %get-tuple-element.772), kind=kOutput, calls=%fused_computation.140.clone.1 | convolution fusion | flops 254803968 | bytes 1806336 | tf_op jit(solution)/shard_map/while/body/eval_jaxpr/dot_general | solution.py:79
  346.3 6.0 %fusion.379 = f32[48,48,2,48,1]{0,3,4,2,1:T(8,128)S(1)} fusion(f32[48,48,2,48,1]{0,1,2,4,3:T(8,128)} %copy.175, f32[48,2,2,48]{3,0,1,2:T(8,128)S(1)} %get-tuple-element.772), kind=kOutput, calls=%fused_computation.144.clone.1 | convolution fusion | flops 254803968 | bytes 1806336 | tf_op jit(solution)/shard_map/while/body/eval_jaxpr/dot_general | solution.py:79
  363.3 6.2 %fusion.369 = f32[48,48,2,48,1]{0,3,4,2,1:T(8,128)S(1)} fusion(f32[48,48,2,48,1]{0,1,2,4,3:T(8,128)} %copy.171, f32[48,2,2,48]{3,0,1,2:T(8,128)S(1)} %get-tuple-element.772), kind=kOutput, calls=%fused_computation.128.clone.1 | convolution fusion | flops 254803968 | bytes 1806336 | tf_op jit(solution)/shard_map/while/body/eval_jaxpr/dot_general | solution.py:79
  371.8 4.2 fusion.384
  386.5 4.4 %all-to-all-start.1 = ((f32[2,48,2304]{2,0,1:T(2,128)}), f32[2,48,2304]{2,0,1:T(2,128)}, u32[]{:S(2)}, u32[]{:S(2)}) async-start(f32[2,48,2304]{2,0,1:T(2,128)} %get-tuple-element.142), calls=%async_computation.1 | async-start | bytes 1769472 | tf_op jit(solution)/shard_map/all_to_all | solution.py:139
  402.2 10.9 %all-to-all-done.1 = f32[2,48,2304]{2,0,1:T(2,128)} async-done(((f32[2,48,2304]{2,0,1:T(2,128)}), f32[2,48,2304]{2,0,1:T(2,128)}, u32[]{:S(2)}, u32[]{:S(2)}) %all-to-all-start.1) | async-done | bytes 884768 | tf_op jit(solution)/shard_map/all_to_all | solution.py:139
  (206 shorter events, 190.8 us)
Async XLA Ops:
  2.8 35.8 %all-to-all-start = ((f32[16,6,2304]{2,1,0:T(8,128)}), f32[16,6,2304]{2,1,0:T(8,128)S(1)}, u32[]{:S(2)}, u32[]{:S(2)}) async-start(f32[16,6,2304]{2,1,0:T(8,128)} %copy.77), calls=%async_computation | async-start | bytes 2359296 | tf_op jit(solution)/shard_map/all_to_all | solution.py:137
  10.0 14.1 %copy-start.31 = (f32[48]{0:T(128)}, f32[48]{0:T(128)S(1)}, u32[]{:S(2)}) copy-start(f32[48]{0:T(128)S(1)} %get-tuple-element.734) | copy-start | bytes 580
  10.6 13.6 %copy-start.21 = (f32[48,48]{1,0:T(8,128)}, f32[48,48]{1,0:T(8,128)S(1)}, u32[]{:S(2)}) copy-start(f32[48,48]{1,0:T(8,128)S(1)} %get-tuple-element.736) | copy-start | bytes 27652
  10.6 13.6 %copy-start.23 = (f32[48,48]{1,0:T(8,128)}, f32[48,48]{1,0:T(8,128)S(1)}, u32[]{:S(2)}) copy-start(f32[48,48]{1,0:T(8,128)S(1)} %get-tuple-element.738) | copy-start | bytes 27652
  10.6 13.6 %copy-start.25 = (f32[48,48]{1,0:T(8,128)}, f32[48,48]{1,0:T(8,128)S(1)}, u32[]{:S(2)}) copy-start(f32[48,48]{1,0:T(8,128)S(1)} %get-tuple-element.735) | copy-start | bytes 27652
  10.6 13.6 %copy-start.27 = (f32[48,48]{1,0:T(8,128)}, f32[48,48]{1,0:T(8,128)S(1)}, u32[]{:S(2)}) copy-start(f32[48,48]{1,0:T(8,128)S(1)} %get-tuple-element.732) | copy-start | bytes 27652
  80.5 3.5 copy-start.6
  80.5 3.5 copy-start.7
  97.4 3.6 copy-start.17
  97.4 3.5 copy-start.18
  97.4 3.5 copy-start.24
  141.2 3.6 copy-start.13
  141.2 3.6 copy-start.14
  141.2 3.6 copy-start.22
  141.2 3.6 copy-start.26
  191.7 8.3 %copy-start.2 = (f32[48,48,2,48]{3,1,2,0:T(8,128)S(1)}, f32[48,48,2,48]{3,1,2,0:T(8,128)}, u32[]{:S(2)}) copy-start(f32[48,48,2,48]{3,1,2,0:T(8,128)} %bitcast_multiply_fusion.41) | copy-start | bytes 2654212 | tf_op jit(solution)/shard_map/while
  191.7 8.3 %copy-start.3 = (f32[48,48,2,48]{3,1,2,0:T(8,128)S(1)}, f32[48,48,2,48]{3,1,2,0:T(8,128)}, u32[]{:S(2)}) copy-start(f32[48,48,2,48]{3,1,2,0:T(8,128)} %bitcast_multiply_fusion.42) | copy-start | bytes 2654212 | tf_op jit(solution)/shard_map/while
  252.0 3.5 copy-start.6
  268.9 3.6 copy-start.17
  269.0 3.5 copy-start.18
  269.0 3.5 copy-start.24
  312.7 3.6 copy-start.13
  312.7 3.6 copy-start.14
  312.7 3.6 copy-start.22
  312.7 3.6 copy-start.26
  363.3 8.3 %copy-start.2 = (f32[48,48,2,48]{3,1,2,0:T(8,128)S(1)}, f32[48,48,2,48]{3,1,2,0:T(8,128)}, u32[]{:S(2)}) copy-start(f32[48,48,2,48]{3,1,2,0:T(8,128)} %bitcast_multiply_fusion.41) | copy-start | bytes 2654212 | tf_op jit(solution)/shard_map/while
  363.3 8.3 %copy-start.3 = (f32[48,48,2,48]{3,1,2,0:T(8,128)S(1)}, f32[48,48,2,48]{3,1,2,0:T(8,128)}, u32[]{:S(2)}) copy-start(f32[48,48,2,48]{3,1,2,0:T(8,128)} %bitcast_multiply_fusion.42) | copy-start | bytes 2654212 | tf_op jit(solution)/shard_map/while
  386.5 4.4 %copy-start.19 = (f32[16,6,2304]{2,0,1:T(8,128)S(1)}, f32[16,6,2304]{2,0,1:T(8,128)}, u32[]{:S(2)}) copy-start(f32[16,6,2304]{2,0,1:T(8,128)} %param.6) | copy-start | bytes 2654212
  386.5 7.1 %copy-start.34 = (s32[64]{0:T(128)S(1)}, s32[64]{0:T(128)}, u32[]{:S(2)}) copy-start(s32[64]{0:T(128)} %param.8) | copy-start | bytes 772
  386.5 26.5 %all-to-all-start.1 = ((f32[2,48,2304]{2,0,1:T(2,128)}), f32[2,48,2304]{2,0,1:T(2,128)}, u32[]{:S(2)}, u32[]{:S(2)}) async-start(f32[2,48,2304]{2,0,1:T(2,128)} %get-tuple-element.142), calls=%async_computation.1 | async-start | bytes 1769472 | tf_op jit(solution)/shard_map/all_to_all | solution.py:139
  391.0 26.1 %collective-permute-start = (f32[1,6,2304]{2,0,1:T(1,128)S(1)}, f32[1,6,2304]{2,0,1:T(1,128)S(1)}, u32[]{:S(2)}, u32[]{:S(2)}) collective-permute-start(f32[1,6,2304]{2,0,1:T(1,128)S(1)} %get-tuple-element.523), channel_id=1, source_target_pairs={{0,8},{8,16},{16,24},{1,9},{9,17},{17,25},{2,10},{10,18},{18,26},{... | collective-permute-start | bytes 165896 | tf_op jit(solution)/shard_map/ppermute | solution.py:31
  392.3 24.9 %collective-permute-start.1 = (f32[1,6,2304]{2,0,1:T(1,128)S(1)}, f32[1,6,2304]{2,0,1:T(1,128)S(1)}, u32[]{:S(2)}, u32[]{:S(2)}) collective-permute-start(f32[1,6,2304]{2,0,1:T(1,128)S(1)} %get-tuple-element.524), channel_id=1, source_target_pairs={{8,0},{16,8},{24,16},{9,1},{17,9},{25,17},{10,2},{18,10},{26,18},{... | collective-permute-start | bytes 165896 | tf_op jit(solution)/shard_map/ppermute | solution.py:33
  (32 other events, 76.8 us)
where the time goes:
time: 423 us; the launch traced here: 419 us
  matrix products  196 us (46%)
  local copies, waits for them, and re-layouts  94.4 us (22%)
  other arithmetic  82.4 us (19%)
  waiting for transfers between devices  25.3 us (6%)
  starting transfers between devices  14.2 us (3%)
  loops' own time  5.61 us (1%)
    dot_general x48, matrix products, apply_table(): lax.dot_general(tensor, table, ((dims, tuple(range(len(dims)))), ((), ())...  196 us
    dot_general x16, local copies, waits for them, and re-layouts, apply_table(): lax.dot_general(tensor, table, ((dims, tuple(range(len(dims)))), ((), ())...  60.6 us
    sub x6, other arithmetic, packed(): joined_real = first_factor * real_part - second_factor * imag_part  58.4 us
    all_to_all x1, waiting for transfers between devices, body(): lax.all_to_all(distribution, 'vel', split_axis=0, concat_axis=1, tiled=True)  14.4 us
    div x1, other arithmetic, kernel_tables(): loss_total = sum(loss_tables) / 6.0  13.5 us
    all_to_all x1, waiting for transfers between devices, body(): lax.all_to_all(cell_terms, 'vel', split_axis=1, concat_axis=0, tiled=True)  10.9 us
  transfers between devices with their start and end apart: 4, of which 2 were waited for; matrix products, arithmetic and copies ran while one was open for 6% of the time, Pallas kernels for 0%

commit v1 on v0

--- a/solution.py
+++ b/solution.py
@@ -18,6 +18,18 @@
     (-GOLDEN, 0.0, 1.0),
 )
 HIGHEST_MODE = lax.Precision.HIGHEST
+
+
+def in_blocks(array, dim, size):
+    shape = array.shape
+    blocks = array.reshape(*shape[:dim], size, shape[dim] // size, *shape[dim + 1 :])
+    return jnp.moveaxis(blocks, dim, 0)
+
+
+def joined_along(tiles, dim):
+    tiles = jnp.moveaxis(tiles, 0, dim)
+    lengths = tiles.shape
+    return tiles.reshape(*lengths[:dim], lengths[dim] * lengths[dim + 1], *lengths[dim + 2 :])
 
 
 def padded_2(cells, sides, width):
@@ -136,7 +148,17 @@
 
     regrouped = lax.all_to_all(distribution, "vel", split_axis=0, concat_axis=1, tiled=True)
     cell_terms = lax.map(from_cell, regrouped)
-    collision_term = lax.all_to_all(cell_terms, "vel", split_axis=1, concat_axis=0, tiled=True)
+    count_2, index_2 = (lax.axis_size("vel"), lax.axis_index("vel"))
+    blocks = in_blocks(cell_terms, 1, count_2)
+    out = blocks
+    for step in range(1, count_2):
+        target, source = ((index_2 + step) % count_2, (index_2 - step) % count_2)
+        sent = lax.dynamic_index_in_dim(blocks, target, 0)
+        received = lax.ppermute(
+            sent, "vel", [(i_2, (i_2 + step) % count_2) for i_2 in range(count_2)]
+        )
+        out = lax.dynamic_update_slice_in_dim(out, received, source, axis=0)
+    collision_term = joined_along(out, 0)
     offset = lax.axis_index("space") * cell_count
     padded = padded_2(distribution, (("space", 0),), 1)
     mirror = distribution.reshape(cell_count, planes_dev, points, points)[:, :, ::-1, :].reshape(

time: 423 us -> 427 us (level)
  starting transfers between devices: 14.2 us -> 22.8 us
  waiting for transfers between devices: 25.3 us -> 17.5 us
    ppermute x0 -> x7, waiting for transfers between devices: none -> 16.2 us  [body(): lax.ppermute(sent, 'vel', [(i_2, (i_2 + step) % count_2) for i_2 in range...]
    all_to_all x1, waiting for transfers between devices: 14.4 us -> 1.33 us  [body(): lax.all_to_all(distribution, 'vel', split_axis=0, concat_axis=1, tiled=True)]
    ppermute x0 -> x7, starting transfers between devices: none -> 12 us  [body(): lax.ppermute(sent, 'vel', [(i_2, (i_2 + step) % count_2) for i_2 in range...]
    all_to_all x1 -> x0, waiting for transfers between devices: 10.9 us -> none  [body(): lax.all_to_all(cell_terms, 'vel', split_axis=1, concat_axis=0, tiled=True)]
    all_to_all x1 -> x0, starting transfers between devices: 4.36 us -> none  [body(): lax.all_to_all(cell_terms, 'vel', split_axis=1, concat_axis=0, tiled=True)]
  transfers between devices with their start and end apart: 4 -> 10, of which waited for: 2 -> 6; matrix products, arithmetic and copies ran while one was open for 6% -> 87% of each run, Pallas kernels for 0% -> 0%
where the time goes in v1:
time: 427 us; the launch traced here: 421 us
  matrix products  196 us (46%)
  local copies, waits for them, and re-layouts  94.1 us (22%)
  other arithmetic  84.3 us (20%)
  starting transfers between devices  22.8 us (5%)
  waiting for transfers between devices  17.5 us (4%)
  loops' own time  4.48 us (1%)
    dot_general x48, matrix products, apply_table(): lax.dot_general(tensor, table, ((dims, tuple(range(len(dims)))), ((), ())...  196 us
    dot_general x16, local copies, waits for them, and re-layouts, apply_table(): lax.dot_general(tensor, table, ((dims, tuple(range(len(dims)))), ((), ())...  60.7 us
    sub x6, other arithmetic, packed(): joined_real = first_factor * real_part - second_factor * imag_part  58.4 us
    ppermute x7, waiting for transfers between devices, body(): lax.ppermute(sent, 'vel', [(i_2, (i_2 + step) % count_2) for i_2 in range...  16.2 us
    div x1, other arithmetic, kernel_tables(): loss_total = sum(loss_tables) / 6.0  13.5 us
    ppermute x7, starting transfers between devices, body(): lax.ppermute(sent, 'vel', [(i_2, (i_2 + step) % count_2) for i_2 in range...  12 us
  transfers between devices with their start and end apart: 10, of which 6 were waited for; matrix products, arithmetic and copies ran while one was open for 87% of the time, Pallas kernels for 0%

profile of v1, /device:TPU:0, one launch (start us, length us, event | category | flops | bytes accessed | tf_op | source)
XLA Modules:
  0.0 420.5 jit_solution(13772094419603681201)
XLA Ops:
  2.8 7.4 %all-to-all-start = ((f32[16,6,2304]{2,1,0:T(8,128)}), f32[16,6,2304]{2,1,0:T(8,128)}, u32[]{:S(2)}, u32[]{:S(2)}) async-start(f32[16,6,2304]{2,1,0:T(8,128)} %copy.84), calls=%async_computation | async-start | bytes 2359296 | tf_op jit(solution)/shard_map/all_to_all | solution.py:149
  23.9 13.5 %add_multiply_fusion = (f32[48,48,48]{2,1,0:T(8,128)}, f32[48,48,48]{2,1,0:T(8,128)}, f32[48,48,48]{2,1,0:T(8,128)}, f32[48,48,48]{2,1,0:T(8,128)}, f32[48,48,48...) fusion(f32[48]{0:T(128)S(1)} %get-tuple-element.744, f32[48,48]{1,0:T(8,128)S(1)} %get-tuple-element.746, ...), kind=kLoop, calls=%fused_computation.329 | loop fusion | flops 26652672 | bytes 3161856 | tf_op jit(solution)/shard_map/div | solution.py:70
  40.6 346.1 %while.13 = (s32[]{:T(128)}, f32[2,48,2304]{2,0,1:T(2,128)}, f32[2,48,2304]{2,0,1:T(2,128)S(1)}, f32[48,2,48]{2,0,1:T(8,128)S(1)}, f32[48,2,2,48]{3,0,1,2:T(8,12...) while((s32[]{:T(128)}, f32[2,48,2304]{2,0,1:T(2,128)}, ...), condition=%wide.region_1.3_spmd.clone.clone.clone, body=%wide.region_0.2_spmd.clone.clone.clone.sunk | while | flops 5998288896 | bytes 128030208 | solution.py:150
  50.4 6.0 %fusion.365 = f32[48,48,2,48,1]{0,3,4,2,1:T(8,128)S(1)} fusion(f32[48,48,2,48,1]{1,0,2,4,3:T(8,128)} %copy.177, f32[48,2,2,48]{3,0,1,2:T(8,128)S(1)} %get-tuple-element.777), kind=kOutput, calls=%fused_computation.156.clone.1 | convolution fusion | flops 254803968 | bytes 1806336 | tf_op jit(solution)/shard_map/while/body/eval_jaxpr/dot_general | solution.py:91
  58.5 9.9 %fusion.367 = (f32[48,48,1,48]{3,1,2,0:T(8,128)}, f32[48,48,1,48]{3,1,2,0:T(8,128)}, f32[48,48,1,48]{3,1,2,0:T(8,128)S(1)}, f32[48,48,1,48]{3,1,2,0:T(8,128)S(1)...) fusion(f32[48,48,48]{2,1,0:T(8,128)S(1)} %copy-done.16, f32[48]{0:T(128)S(1)} %get-tuple-element.786, ...), kind=kLoop, calls=%fused_computation.117.clone.1 | loop fusion | flops 2211840 | bytes 4884672 | tf_op jit(solution)/shard_map/while/body/eval_jaxpr/sub | solution.py:122
  75.9 6.0 %fusion.381 = f32[48,48,2,48,1]{0,3,4,2,1:T(8,128)S(1)} fusion(f32[48,48,2,48,1]{0,1,2,4,3:T(8,128)} %copy.183, f32[48,2,2,48]{3,0,1,2:T(8,128)S(1)} %get-tuple-element.779), kind=kOutput, calls=%fused_computation.148.clone.1 | convolution fusion | flops 254803968 | bytes 1806336 | tf_op jit(solution)/shard_map/while/body/eval_jaxpr/dot_general | solution.py:91
  92.9 6.0 %fusion.383 = f32[48,48,2,48,1]{0,3,4,2,1:T(8,128)S(1)} fusion(f32[48,48,2,48,1]{0,1,2,4,3:T(8,128)} %copy.184, f32[48,2,2,48]{3,0,1,2:T(8,128)S(1)} %get-tuple-element.779), kind=kOutput, calls=%fused_computation.152.clone.1 | convolution fusion | flops 254803968 | bytes 1806336 | tf_op jit(solution)/shard_map/while/body/eval_jaxpr/dot_general | solution.py:91
  102.4 9.6 %fusion.370 = (f32[48,48,1,48]{3,1,2,0:T(8,128)}, f32[48,48,1,48]{3,1,2,0:T(8,128)}, f32[48,48,1,48]{3,1,2,0:T(8,128)S(1)}, f32[48,48,1,48]{3,1,2,0:T(8,128)S(1)}) fusion(f32[48,48,48]{2,1,0:T(8,128)S(1)} %copy-done.18, f32[48]{0:T(128)S(1)} %get-tuple-element.792, f32[48,48]{1,0:T(8,128)S(1)} %copy-done.28, f32[48,48,2,48]{3,1,2,0:T(8,128)S(1)} %fusion.366, ...), kind=kLoop, calls=%fused_computation.93.clone.1 | loop fusion | flops 1769472 | bytes 3557568 | tf_op jit(solution)/shard_map/while/body/eval_jaxpr/sub | solution.py:122
  119.6 6.0 %fusion.372 = f32[48,48,2,48,1]{0,3,4,2,1:T(8,128)S(1)} fusion(f32[48,48,2,48,1]{0,1,2,4,3:T(8,128)} %copy.179, f32[48,2,2,48]{3,0,1,2:T(8,128)S(1)} %get-tuple-element.779), kind=kOutput, calls=%fused_computation.132.clone.1 | convolution fusion | flops 254803968 | bytes 1806336 | tf_op jit(solution)/shard_map/while/body/eval_jaxpr/dot_general | solution.py:91
  132.6 4.1 copy.180
  136.8 6.0 %fusion.374 = f32[48,48,2,48,1]{0,3,4,2,1:T(8,128)S(1)} fusion(f32[48,48,2,48,1]{0,1,2,4,3:T(8,128)} %copy.180, f32[48,2,2,48]{3,0,1,2:T(8,128)S(1)} %get-tuple-element.779), kind=kOutput, calls=%fused_computation.136.clone.1 | convolution fusion | flops 254803968 | bytes 1806336 | tf_op jit(solution)/shard_map/while/body/eval_jaxpr/dot_general | solution.py:91
  146.4 9.6 %fusion.375 = (f32[48,48,1,48]{3,1,2,0:T(8,128)}, f32[48,48,1,48]{3,1,2,0:T(8,128)}, f32[48,48,1,48]{3,1,2,0:T(8,128)S(1)}, f32[48,48,1,48]{3,1,2,0:T(8,128)S(1)}) fusion(f32[48,48,48]{2,1,0:T(8,128)S(1)} %copy-done.14, f32[48]{0:T(128)S(1)} %get-tuple-element.789, f32[48,48]{1,0:T(8,128)S(1)} %copy-done.30, f32[48,48,2,48]{3,1,2,0:T(8,128)S(1)} %fusion.366, ...), kind=kLoop, calls=%fused_computation.105.clone.1 | loop fusion | flops 1769472 | bytes 3557568 | tf_op jit(solution)/shard_map/while/body/eval_jaxpr/sub | solution.py:122
  160.8 6.0 %fusion.377 = f32[48,48,2,48,1]{0,3,4,2,1:T(8,128)S(1)} fusion(f32[48,48,2,48,1]{0,1,2,4,3:T(8,128)} %copy.181, f32[48,2,2,48]{3,0,1,2:T(8,128)S(1)} %get-tuple-element.779), kind=kOutput, calls=%fused_computation.140.clone.1 | convolution fusion | flops 254803968 | bytes 1806336 | tf_op jit(solution)/shard_map/while/body/eval_jaxpr/dot_general | solution.py:91
  176.3 6.0 %fusion.379 = f32[48,48,2,48,1]{0,3,4,2,1:T(8,128)S(1)} fusion(f32[48,48,2,48,1]{0,1,2,4,3:T(8,128)} %copy.182, f32[48,2,2,48]{3,0,1,2:T(8,128)S(1)} %get-tuple-element.779), kind=kOutput, calls=%fused_computation.144.clone.1 | convolution fusion | flops 254803968 | bytes 1806336 | tf_op jit(solution)/shard_map/while/body/eval_jaxpr/dot_general | solution.py:91
  193.2 6.2 %fusion.369 = f32[48,48,2,48,1]{0,3,4,2,1:T(8,128)S(1)} fusion(f32[48,48,2,48,1]{0,1,2,4,3:T(8,128)} %copy.178, f32[48,2,2,48]{3,0,1,2:T(8,128)S(1)} %get-tuple-element.779), kind=kOutput, calls=%fused_computation.128.clone.1 | convolution fusion | flops 254803968 | bytes 1806336 | tf_op jit(solution)/shard_map/while/body/eval_jaxpr/dot_general | solution.py:91
  201.8 4.1 fusion.384
  221.9 6.0 %fusion.365 = f32[48,48,2,48,1]{0,3,4,2,1:T(8,128)S(1)} fusion(f32[48,48,2,48,1]{1,0,2,4,3:T(8,128)} %copy.177, f32[48,2,2,48]{3,0,1,2:T(8,128)S(1)} %get-tuple-element.777), kind=kOutput, calls=%fused_computation.156.clone.1 | convolution fusion | flops 254803968 | bytes 1806336 | tf_op jit(solution)/shard_map/while/body/eval_jaxpr/dot_general | solution.py:91
  230.0 9.9 %fusion.367 = (f32[48,48,1,48]{3,1,2,0:T(8,128)}, f32[48,48,1,48]{3,1,2,0:T(8,128)}, f32[48,48,1,48]{3,1,2,0:T(8,128)S(1)}, f32[48,48,1,48]{3,1,2,0:T(8,128)S(1)...) fusion(f32[48,48,48]{2,1,0:T(8,128)S(1)} %copy-done.16, f32[48]{0:T(128)S(1)} %get-tuple-element.786, ...), kind=kLoop, calls=%fused_computation.117.clone.1 | loop fusion | flops 2211840 | bytes 4884672 | tf_op jit(solution)/shard_map/while/body/eval_jaxpr/sub | solution.py:122
  247.4 6.0 %fusion.381 = f32[48,48,2,48,1]{0,3,4,2,1:T(8,128)S(1)} fusion(f32[48,48,2,48,1]{0,1,2,4,3:T(8,128)} %copy.183, f32[48,2,2,48]{3,0,1,2:T(8,128)S(1)} %get-tuple-element.779), kind=kOutput, calls=%fused_computation.148.clone.1 | convolution fusion | flops 254803968 | bytes 1806336 | tf_op jit(solution)/shard_map/while/body/eval_jaxpr/dot_general | solution.py:91
  264.4 6.0 %fusion.383 = f32[48,48,2,48,1]{0,3,4,2,1:T(8,128)S(1)} fusion(f32[48,48,2,48,1]{0,1,2,4,3:T(8,128)} %copy.184, f32[48,2,2,48]{3,0,1,2:T(8,128)S(1)} %get-tuple-element.779), kind=kOutput, calls=%fused_computation.152.clone.1 | convolution fusion | flops 254803968 | bytes 1806336 | tf_op jit(solution)/shard_map/while/body/eval_jaxpr/dot_general | solution.py:91
  274.0 9.6 %fusion.370 = (f32[48,48,1,48]{3,1,2,0:T(8,128)}, f32[48,48,1,48]{3,1,2,0:T(8,128)}, f32[48,48,1,48]{3,1,2,0:T(8,128)S(1)}, f32[48,48,1,48]{3,1,2,0:T(8,128)S(1)}) fusion(f32[48,48,48]{2,1,0:T(8,128)S(1)} %copy-done.18, f32[48]{0:T(128)S(1)} %get-tuple-element.792, f32[48,48]{1,0:T(8,128)S(1)} %copy-done.28, f32[48,48,2,48]{3,1,2,0:T(8,128)S(1)} %fusion.366, ...), kind=kLoop, calls=%fused_computation.93.clone.1 | loop fusion | flops 1769472 | bytes 3557568 | tf_op jit(solution)/shard_map/while/body/eval_jaxpr/sub | solution.py:122
  287.1 4.3 %copy.179 = f32[48,48,2,48,1]{0,1,2,4,3:T(8,128)} copy(f32[48,48,2,48,1]{3,1,2,0,4:T(8,128)} %fusion.371) | data formatting | bytes 1769472 | tf_op jit(solution)/shard_map/while/body/eval_jaxpr/dot_general | solution.py:91
  291.3 6.0 %fusion.372 = f32[48,48,2,48,1]{0,3,4,2,1:T(8,128)S(1)} fusion(f32[48,48,2,48,1]{0,1,2,4,3:T(8,128)} %copy.179, f32[48,2,2,48]{3,0,1,2:T(8,128)S(1)} %get-tuple-element.779), kind=kOutput, calls=%fused_computation.132.clone.1 | convolution fusion | flops 254803968 | bytes 1806336 | tf_op jit(solution)/shard_map/while/body/eval_jaxpr/dot_general | solution.py:91
  308.2 6.0 %fusion.374 = f32[48,48,2,48,1]{0,3,4,2,1:T(8,128)S(1)} fusion(f32[48,48,2,48,1]{0,1,2,4,3:T(8,128)} %copy.180, f32[48,2,2,48]{3,0,1,2:T(8,128)S(1)} %get-tuple-element.779), kind=kOutput, calls=%fused_computation.136.clone.1 | convolution fusion | flops 254803968 | bytes 1806336 | tf_op jit(solution)/shard_map/while/body/eval_jaxpr/dot_general | solution.py:91
  317.9 9.6 %fusion.375 = (f32[48,48,1,48]{3,1,2,0:T(8,128)}, f32[48,48,1,48]{3,1,2,0:T(8,128)}, f32[48,48,1,48]{3,1,2,0:T(8,128)S(1)}, f32[48,48,1,48]{3,1,2,0:T(8,128)S(1)}) fusion(f32[48,48,48]{2,1,0:T(8,128)S(1)} %copy-done.14, f32[48]{0:T(128)S(1)} %get-tuple-element.789, f32[48,48]{1,0:T(8,128)S(1)} %copy-done.30, f32[48,48,2,48]{3,1,2,0:T(8,128)S(1)} %fusion.366, ...), kind=kLoop, calls=%fused_computation.105.clone.1 | loop fusion | flops 1769472 | bytes 3557568 | tf_op jit(solution)/shard_map/while/body/eval_jaxpr/sub | solution.py:122
  332.3 6.0 %fusion.377 = f32[48,48,2,48,1]{0,3,4,2,1:T(8,128)S(1)} fusion(f32[48,48,2,48,1]{0,1,2,4,3:T(8,128)} %copy.181, f32[48,2,2,48]{3,0,1,2:T(8,128)S(1)} %get-tuple-element.779), kind=kOutput, calls=%fused_computation.140.clone.1 | convolution fusion | flops 254803968 | bytes 1806336 | tf_op jit(solution)/shard_map/while/body/eval_jaxpr/dot_general | solution.py:91
  347.9 6.0 %fusion.379 = f32[48,48,2,48,1]{0,3,4,2,1:T(8,128)S(1)} fusion(f32[48,48,2,48,1]{0,1,2,4,3:T(8,128)} %copy.182, f32[48,2,2,48]{3,0,1,2:T(8,128)S(1)} %get-tuple-element.779), kind=kOutput, calls=%fused_computation.144.clone.1 | convolution fusion | flops 254803968 | bytes 1806336 | tf_op jit(solution)/shard_map/while/body/eval_jaxpr/dot_general | solution.py:91
  364.8 6.2 %fusion.369 = f32[48,48,2,48,1]{0,3,4,2,1:T(8,128)S(1)} fusion(f32[48,48,2,48,1]{0,1,2,4,3:T(8,128)} %copy.178, f32[48,2,2,48]{3,0,1,2:T(8,128)S(1)} %get-tuple-element.779), kind=kOutput, calls=%fused_computation.128.clone.1 | convolution fusion | flops 254803968 | bytes 1806336 | tf_op jit(solution)/shard_map/while/body/eval_jaxpr/dot_general | solution.py:91
  373.4 4.1 fusion.384
  392.5 4.2 collective-permute-done.2
  397.9 8.2 %collective-permute-done.4 = f32[1,2,6,2304]{3,1,2,0:T(2,128)S(1)} collective-permute-done((f32[1,2,6,2304]{3,1,2,0:T(2,128)S(1)}, f32[1,2,6,2304]{3,1,2,0:T(2,128)S(1)}, u32[]{:S(2)}, u32[]{:S(2)}) %collective-permute-start.4) | collective-permute-done | bytes 110624 | tf_op jit(solution)/shard_map/ppermute | solution.py:157
  406.1 4.5 %collective-permute-start.7 = (f32[1,2,6,2304]{3,1,2,0:T(2,128)S(1)}, f32[1,2,6,2304]{3,1,2,0:T(2,128)S(1)}, u32[]{:S(2)}, u32[]{:S(2)}) collective-permute-start(f32[1,2,6,2304]{3,1,2,0:T(2,128)S(1)} %get-tuple-element.524), channel_id=1, source_target_pairs={{0,6},{1,7},{2,0},{3,1},{4,2},{5,3},{6,4},{7,5},{8,14},{9,15},{10,... | collective-permute-start | bytes 331784 | tf_op jit(solution)/shard_map/ppermute | solution.py:157
  (230 shorter events, 205.8 us)
Async XLA Ops:
  2.7 7.4 %copy-start.19 = (f32[16,6,2304]{2,0,1:T(8,128)S(1)}, f32[16,6,2304]{2,0,1:T(8,128)}, u32[]{:S(2)}) copy-start(f32[16,6,2304]{2,0,1:T(8,128)} %param.6) | copy-start | bytes 2654212
  2.8 36.1 %all-to-all-start = ((f32[16,6,2304]{2,1,0:T(8,128)}), f32[16,6,2304]{2,1,0:T(8,128)}, u32[]{:S(2)}, u32[]{:S(2)}) async-start(f32[16,6,2304]{2,1,0:T(8,128)} %copy.84), calls=%async_computation | async-start | bytes 2359296 | tf_op jit(solution)/shard_map/all_to_all | solution.py:149
  10.9 406.3 %collective-permute-start = (f32[1,6,2304]{2,0,1:T(1,128)}, f32[1,6,2304]{2,0,1:T(1,128)}, u32[]{:S(2)}, u32[]{:S(2)}) collective-permute-start(f32[1,6,2304]{2,0,1:T(1,128)} %get-tuple-element.530), channel_id=1, source_target_pairs={{0,8},{8,16},{16,24},{1,9},{9,17},{17,25},{2,10},{10,18},{18,26},{... | collective-permute-start | bytes 165896 | tf_op jit(solution)/shard_map/ppermute | solution.py:43
  12.9 404.3 %collective-permute-start.1 = (f32[1,6,2304]{2,0,1:T(1,128)}, f32[1,6,2304]{2,0,1:T(1,128)}, u32[]{:S(2)}, u32[]{:S(2)}) collective-permute-start(f32[1,6,2304]{2,0,1:T(1,128)} %get-tuple-element.531), channel_id=1, source_target_pairs={{8,0},{16,8},{24,16},{9,1},{17,9},{25,17},{10,2},{18,10},{26,18},{... | collective-permute-start | bytes 165896 | tf_op jit(solution)/shard_map/ppermute | solution.py:45
  14.2 9.7 %copy-start.34 = (f32[48]{0:T(128)}, f32[48]{0:T(128)S(1)}, u32[]{:S(2)}) copy-start(f32[48]{0:T(128)S(1)} %get-tuple-element.741) | copy-start | bytes 580
  23.9 13.6 %copy-start.25 = (f32[48,48]{1,0:T(8,128)}, f32[48,48]{1,0:T(8,128)S(1)}, u32[]{:S(2)}) copy-start(f32[48,48]{1,0:T(8,128)S(1)} %get-tuple-element.743) | copy-start | bytes 27652
  23.9 13.6 %copy-start.27 = (f32[48,48]{1,0:T(8,128)}, f32[48,48]{1,0:T(8,128)S(1)}, u32[]{:S(2)}) copy-start(f32[48,48]{1,0:T(8,128)S(1)} %get-tuple-element.745) | copy-start | bytes 27652
  23.9 13.6 %copy-start.29 = (f32[48,48]{1,0:T(8,128)}, f32[48,48]{1,0:T(8,128)S(1)}, u32[]{:S(2)}) copy-start(f32[48,48]{1,0:T(8,128)S(1)} %get-tuple-element.742) | copy-start | bytes 27652
  23.9 13.6 %copy-start.31 = (f32[48,48]{1,0:T(8,128)}, f32[48,48]{1,0:T(8,128)S(1)}, u32[]{:S(2)}) copy-start(f32[48,48]{1,0:T(8,128)S(1)} %get-tuple-element.739) | copy-start | bytes 27652
  98.9 3.6 copy-start.17
  98.9 3.6 copy-start.18
  142.8 3.6 copy-start.13
  142.8 3.6 copy-start.14
  142.8 3.6 copy-start.26
  142.8 3.6 copy-start.30
  193.2 8.3 %copy-start.2 = (f32[48,48,2,48]{3,1,2,0:T(8,128)S(1)}, f32[48,48,2,48]{3,1,2,0:T(8,128)}, u32[]{:S(2)}) copy-start(f32[48,48,2,48]{3,1,2,0:T(8,128)} %bitcast_multiply_fusion.41) | copy-start | bytes 2654212 | tf_op jit(solution)/shard_map/while
  193.2 8.3 %copy-start.3 = (f32[48,48,2,48]{3,1,2,0:T(8,128)S(1)}, f32[48,48,2,48]{3,1,2,0:T(8,128)}, u32[]{:S(2)}) copy-start(f32[48,48,2,48]{3,1,2,0:T(8,128)} %bitcast_multiply_fusion.42) | copy-start | bytes 2654212 | tf_op jit(solution)/shard_map/while
  270.4 3.6 copy-start.17
  314.2 3.6 copy-start.13
  314.3 3.6 copy-start.14
  314.3 3.6 copy-start.26
  314.3 3.6 copy-start.30
  364.8 8.3 %copy-start.2 = (f32[48,48,2,48]{3,1,2,0:T(8,128)S(1)}, f32[48,48,2,48]{3,1,2,0:T(8,128)}, u32[]{:S(2)}) copy-start(f32[48,48,2,48]{3,1,2,0:T(8,128)} %bitcast_multiply_fusion.41) | copy-start | bytes 2654212 | tf_op jit(solution)/shard_map/while
  364.8 8.3 %copy-start.3 = (f32[48,48,2,48]{3,1,2,0:T(8,128)S(1)}, f32[48,48,2,48]{3,1,2,0:T(8,128)}, u32[]{:S(2)}) copy-start(f32[48,48,2,48]{3,1,2,0:T(8,128)} %bitcast_multiply_fusion.42) | copy-start | bytes 2654212 | tf_op jit(solution)/shard_map/while
  386.6 10.0 %copy-start.24 = (f32[2,48,2304]{2,0,1:T(2,128)S(1)}, f32[2,48,2304]{2,0,1:T(2,128)}, u32[]{:S(2)}) copy-start(f32[2,48,2304]{2,0,1:T(2,128)} %get-tuple-element.142) | copy-start | bytes 2654212
  388.0 8.7 %collective-permute-start.2 = (f32[1,2,6,2304]{3,1,2,0:T(2,128)S(1)}, f32[1,2,6,2304]{3,1,2,0:T(2,128)S(1)}, u32[]{:S(2)}, u32[]{:S(2)}) collective-permute-start(f32[1,2,6,2304]{3,1,2,0:T(2,128)S(1)} %get-tuple-element.529), channel_id=1, source_target_pairs={{0,1},{1,2},{2,3},{3,4},{4,5},{5,6},{6,7},{7,0},{8,9},{9,10},{10,1... | collective-permute-start | bytes 331784 | tf_op jit(solution)/shard_map/ppermute | solution.py:157
  389.5 7.6 %collective-permute-start.3 = (f32[1,2,6,2304]{3,1,2,0:T(2,128)S(1)}, f32[1,2,6,2304]{3,1,2,0:T(2,128)S(1)}, u32[]{:S(2)}, u32[]{:S(2)}) collective-permute-start(f32[1,2,6,2304]{3,1,2,0:T(2,128)S(1)} %get-tuple-element.528), channel_id=1, source_target_pairs={{0,2},{1,3},{2,4},{3,5},{4,6},{5,7},{6,0},{7,1},{8,10},{9,11},{10,... | collective-permute-start | bytes 331784 | tf_op jit(solution)/shard_map/ppermute | solution.py:157
  390.1 16.0 %collective-permute-start.4 = (f32[1,2,6,2304]{3,1,2,0:T(2,128)S(1)}, f32[1,2,6,2304]{3,1,2,0:T(2,128)S(1)}, u32[]{:S(2)}, u32[]{:S(2)}) collective-permute-start(f32[1,2,6,2304]{3,1,2,0:T(2,128)S(1)} %get-tuple-element.527), channel_id=1, source_target_pairs={{0,3},{1,4},{2,5},{3,6},{4,7},{5,0},{6,1},{7,2},{8,11},{9,12},{10,... | collective-permute-start | bytes 331784 | tf_op jit(solution)/shard_map/ppermute | solution.py:157
  396.7 14.0 %collective-permute-start.5 = (f32[1,2,6,2304]{3,1,2,0:T(2,128)S(1)}, f32[1,2,6,2304]{3,1,2,0:T(2,128)S(1)}, u32[]{:S(2)}, u32[]{:S(2)}) collective-permute-start(f32[1,2,6,2304]{3,1,2,0:T(2,128)S(1)} %get-tuple-element.526), channel_id=1, source_target_pairs={{0,4},{1,5},{2,6},{3,7},{4,0},{5,1},{6,2},{7,3},{8,12},{9,13},{10,... | collective-permute-start | bytes 331784 | tf_op jit(solution)/shard_map/ppermute | solution.py:157
  397.1 15.9 %collective-permute-start.6 = (f32[1,2,6,2304]{3,1,2,0:T(2,128)S(1)}, f32[1,2,6,2304]{3,1,2,0:T(2,128)S(1)}, u32[]{:S(2)}, u32[]{:S(2)}) collective-permute-start(f32[1,2,6,2304]{3,1,2,0:T(2,128)S(1)} %get-tuple-element.525), channel_id=1, source_target_pairs={{0,5},{1,6},{2,7},{3,0},{4,1},{5,2},{6,3},{7,4},{8,13},{9,14},{10,... | collective-permute-start | bytes 331784 | tf_op jit(solution)/shard_map/ppermute | solution.py:157
  406.1 7.2 %collective-permute-start.7 = (f32[1,2,6,2304]{3,1,2,0:T(2,128)S(1)}, f32[1,2,6,2304]{3,1,2,0:T(2,128)S(1)}, u32[]{:S(2)}, u32[]{:S(2)}) collective-permute-start(f32[1,2,6,2304]{3,1,2,0:T(2,128)S(1)} %get-tuple-element.524), channel_id=1, source_target_pairs={{0,6},{1,7},{2,0},{3,1},{4,2},{5,3},{6,4},{7,5},{8,14},{9,15},{10,... | collective-permute-start | bytes 331784 | tf_op jit(solution)/shard_map/ppermute | solution.py:157
  410.6 5.8 %collective-permute-start.8 = (f32[1,2,6,2304]{3,1,2,0:T(2,128)S(1)}, f32[1,2,6,2304]{3,1,2,0:T(2,128)S(1)}, u32[]{:S(2)}, u32[]{:S(2)}) collective-permute-start(f32[1,2,6,2304]{3,1,2,0:T(2,128)S(1)} %get-tuple-element.523), channel_id=1, source_target_pairs={{0,7},{1,0},{2,1},{3,2},{4,3},{5,4},{6,5},{7,6},{8,15},{9,8},{10,9... | collective-permute-start | bytes 331784 | tf_op jit(solution)/shard_map/ppermute | solution.py:157
  (40 other events, 102.2 us)
